TPU v7x, 128 devices: a whole 4x4x4 slice. The times are simulated.
128 devices in a mesh: seq: 8 (over z, core), head: 16 (over y, x).
Axes of the slice: x: 4, y: 4, z: 4, core: 2. Of those that a mesh axis runs over, the one named last changes fastest.
Arguments:
- query: bfloat16 [65536, 2048], P('seq', 'head'), may hold values from -4.5 to 4.5
- keys: bfloat16 [65536, 2048], P('seq', 'head'), may hold values from -4.5 to 4.5
- values: bfloat16 [65536, 2048], P('seq', 'head'), may hold values from -6 to 6
- mem_init: float32 [16, 128, 128], P('head'), may hold values from -362.03867 to 362.03867
- beta: float32 [16], P('head'), may hold values from -2 to 2
- mem_gain: float32 [2048], P('head'), may hold values from 0.1 to 1.9
- loc_gain: float32 [2048], P('head'), may hold values from 0.1 to 1.9
- w_out: bfloat16 [2048, 2048], P('head'), may hold values from -0.125 to 0.125
Outputs:
- attn_out: bfloat16 [65536, 2048], P(('seq', 'head'))
- memory_prefix: float32 [8, 16, 128, 128], P('seq', 'head')
All inputs are finite; a program needn't handle non-finite values.
Results may differ from a plain program's by a relative error of at most 0.0054.
Values may be sent and summed in bfloat16 or wider, within the bound.
A program may use at most 128 MiB of HBM per device.

v0:
```python
import functools
import math

import jax
import jax.numpy as jnp
from jax import lax
from jax.experimental import pallas as pl
from jax.experimental.pallas import tpu as pltpu
from jax.sharding import PartitionSpec as P

HD = 128
SEG = 2048
BLK = 512
D = 2048
NSEG = 4
NX = 4
EPS = 1e-06
MESH = pl.DeviceIdType.MESH
F32 = jnp.float32
BF16 = jnp.bfloat16
C2 = HD**-0.5 * math.log2(math.e)


def gray(t):
    return t + (t // 2) * (1 - 2 * lax.rem(t, 2))


def attend(b, base, q_ref, k_ref, v_ref, s_ref, acc_ref):
    half = BLK // 2
    q = q_ref[pl.ds(pl.multiple_of(base + b * BLK, BLK), BLK), :]

    def score(row0, rows, key0, cols, masked):
        k = k_ref[pl.ds(pl.multiple_of(base + key0, 256), cols), :]
        s = lax.dot_general(
            q[row0 : row0 + rows], k, (((1,), (1,)), ((), ())), preferred_element_type=F32
        )
        s = s * C2
        if masked:
            col = lax.broadcasted_iota(jnp.int32, (rows, cols), 1) + (key0 - b * BLK)
            row = lax.broadcasted_iota(jnp.int32, (rows, cols), 0) + row0
            s = jnp.where(col <= row, s, -jnp.inf)
        s_ref[row0 : row0 + rows, key0 : key0 + cols] = s
        top = s[:, 0:128]
        for t in range(1, cols // 128):
            top = jnp.maximum(top, s[:, t * 128 : (t + 1) * 128])
        return top

    tops = [None, None]

    def merge(i, top):
        tops[i] = top if tops[i] is None else jnp.maximum(tops[i], top)

    for key0 in range(0, b * BLK, BLK):
        top = score(0, BLK, key0, BLK, False)
        merge(0, top[:half])
        merge(1, top[half:])
    merge(1, score(half, half, b * BLK, half, False))
    merge(0, score(0, half, b * BLK, half, True))
    merge(1, score(half, half, b * BLK + half, half, True))
    for i in range(2):
        largest = jnp.max(tops[i], axis=1, keepdims=True)
        length = b * BLK + (i + 1) * half
        rows = slice(i * half, (i + 1) * half)
        p = jnp.exp2(s_ref[rows, 0:length] - largest).astype(BF16)
        v = v_ref[pl.ds(pl.multiple_of(base, SEG), length), :]
        v = jnp.concatenate([v, jnp.ones((length, HD), BF16)], axis=1)
        acc_ref[rows, :] = jnp.dot(p, v, preferred_element_type=F32)


def feature(x):
    x = x.astype(F32)
    return jnp.where(x > 0, x + 1.0, jnp.exp(x)).astype(BF16)


def kernel(
    beta_ref, q_hbm, k_hbm, v_hbm, init_ref, mg_ref, lg_ref, w_hbm,
    out_hbm, prefix_ref,
    q_ref, k_ref, v_ref, kv_ref, tot_ref, trecv, base_ref, memcat, s_ref, acc_ref,
    ho, recv, w4, oacc, o_ref,
    lsem, wsem, osem,
    a_s, a_r, b_s, b_r, z_s, z_r, c_s, c_r, t_s, t_r, h_s, h_r,
):
    s = lax.axis_index("seq")
    h = lax.axis_index("head")
    z, c = s // 2, lax.rem(s, 2)
    y, x = h // NX, lax.rem(h, NX)
    par = lax.rem(z, 2)

    def at(v, d):
        return lax.rem(v + d, NX)

    def head_dev(dy, dx):
        return (s, at(y, dy) * NX + at(x, dx))

    def z_dev(d):
        return (at(z, d) * 2 + c, h)

    mate = (z * 2 + (1 - c), h)

    def remote(src, dst, ssem, rsem, dev):
        return pltpu.make_async_remote_copy(
            src_ref=src, dst_ref=dst, send_sem=ssem, recv_sem=rsem,
            device_id=dev, device_id_type=MESH,
        )

    def rows_of(p, half):
        return pl.ds(pl.multiple_of((2 * p + c) * 32 + 16 * half, 16), 16)

    barrier = pltpu.get_barrier_semaphore()

    def greet_head(i, carry):
        pl.semaphore_signal(
            barrier, inc=1, device_id=(s, lax.rem(h + i, 16)), device_id_type=MESH
        )
        return carry

    lax.fori_loop(1, 16, greet_head, 0)

    def greet_seq(i, carry):
        pl.semaphore_signal(
            barrier, inc=1, device_id=(lax.rem(s + i, 8), h), device_id_type=MESH
        )
        return carry

    lax.fori_loop(1, 8, greet_seq, 0)

    def load(which, n):
        src = (k_hbm, v_hbm, q_hbm)[which]
        dst = (k_ref, v_ref, q_ref)[which]
        span = pl.ds(n * SEG, SEG)
        return pltpu.make_async_copy(src.at[span], dst.at[span], lsem.at[which * NSEG + n])

    for n in range(NSEG):
        load(0, n).start()
        load(1, n).start()
    own = [
        pltpu.make_async_copy(
            w_hbm.at[rows_of(par, half)], w4.at[y, x, rows_of(par, half), :], wsem.at[half]
        )
        for half in range(2)
    ]
    for copy in own:
        copy.start()
    for n in range(NSEG):
        load(2, n).start()

    def stage_a(i):
        half, d = i // 3, i % 3 + 1
        dev = head_dev(0, d) if half == 0 else head_dev(d, 0)
        return remote(
            w_hbm.at[rows_of(par, half)], w4.at[y, x, rows_of(par, half), :],
            a_s.at[i], a_r.at[i], dev,
        )

    def chunk(half, place, p):
        if half == 0:
            return w4.at[place, :, rows_of(p, 0), :]
        return w4.at[:, place, rows_of(p, 1), :]

    def stage_b(i):
        half, d = i // 3, i % 3 + 1
        ref = chunk(half, y if half == 0 else x, par)
        dev = head_dev(d, 0) if half == 0 else head_dev(0, d)
        return remote(ref, ref, b_s.at[i], b_r.at[i], dev)

    def place_of(half, d):
        return at(y if half == 0 else x, NX - d)

    def stage_z(half, d):
        ref = chunk(half, place_of(half, d), par)
        return remote(
            ref, ref, z_s.at[half * 4 + d], z_r.at[half * 4 + d], z_dev(1 if half == 0 else 3)
        )

    def stage_c(kind, half, d):
        ref = chunk(half, place_of(half, d), par if kind == 0 else 1 - par)
        i = kind * 8 + half * 4 + d
        return remote(ref, ref, c_s.at[i], c_r.at[i], mate)

    def prefix_send(d):
        return remote(
            tot_ref, trecv.at[d - 1], t_s.at[d - 1], t_r.at[d - 1], (lax.rem(s + d, 8), h)
        )

    def kv_term(n):
        load(0, n).wait()
        load(1, n).wait()
        span = slice(n * SEG, (n + 1) * SEG)
        kv_ref[n] = lax.dot_general(
            feature(k_ref[span, :]), v_ref[span, :], (((0,), (0,)), ((), ())),
            preferred_element_type=F32,
        )

    kv_term(0)
    pl.semaphore_wait(barrier, 22)
    for i in (0, 2, 3, 5, 1, 4):
        stage_a(i).start()
    for n in range(1, NSEG):
        kv_term(n)
    tot_ref[...] = (kv_ref[0] + kv_ref[1]) + (kv_ref[2] + kv_ref[3])
    for d in range(1, 8):

        @pl.when(s + d < 8)
        def _(d=d):
            prefix_send(d).start()

    for copy in own:
        copy.wait()
    for i in range(6):
        stage_a(i).wait_recv()
    for i in (0, 3, 2, 5, 1, 4):
        stage_b(i).start()
    for half in range(2):
        stage_z(half, 0).start()
        stage_c(0, half, 0).start()
    for n in range(NSEG):
        load(2, n).wait()

    gate = 1.0 / (1.0 + jnp.exp(-jnp.full((1, HD), beta_ref[0], F32)))
    mem_scale = gate * mg_ref[...]
    loc_scale = (1.0 - gate) * lg_ref[...]

    def step(k, carry):
        dy, dx = gray(3 - k // NX), gray(3 - lax.rem(k, NX))
        n, b = at(y, dy), at(x, dx)
        base = pl.multiple_of(n * SEG, SEG)
        for bb in range(4):

            @pl.when(b == bb)
            def _(bb=bb):
                attend(bb, base, q_ref, k_ref, v_ref, s_ref, acc_ref)

        @pl.when(k == 0)
        def _():
            base_ref[...] = init_ref[0]
            for d in range(1, 8):

                @pl.when(s - d >= 0)
                def _(d=d):
                    prefix_send(d).wait_recv()
                    base_ref[...] += trecv[d - 1]

            running = base_ref[...]
            prefix_ref[0, 0] = running * (NSEG * SEG) ** -0.5
            for m in range(NSEG):
                top = running.astype(BF16)
                memcat[m, 0:HD, :] = top
                memcat[m, HD : 2 * HD, :] = (running - top.astype(F32)).astype(BF16)
                if m < NSEG - 1:
                    running = running + kv_ref[m]

        feat = feature(q_ref[pl.ds(pl.multiple_of(base + b * BLK, BLK), BLK), :])
        read = jnp.dot(
            jnp.concatenate([feat, feat], axis=1), memcat[n], preferred_element_type=F32
        )
        read_sq = jnp.mean(read * read, axis=-1, keepdims=True)
        total = acc_ref[:, 0:HD]
        weight = acc_ref[:, HD : HD + 1]
        total_sq = jnp.mean(total * total, axis=-1, keepdims=True)
        mixed = (read * lax.rsqrt(read_sq + EPS)) * mem_scale + (
            total * lax.rsqrt(total_sq + EPS * (weight * weight))
        ) * loc_scale
        mixed = mixed.astype(BF16)

        @pl.when(k < 15)
        def _():
            ho[k] = mixed
            send_block(k).start()

        @pl.when(k == 15)
        def _():
            recv[15] = mixed

        @pl.when(k == 5)
        def _():
            for half in range(2):
                for d in (1, 3):
                    stage_b(half * 3 + d - 1).wait_recv()
                    stage_z(half, d).start()
                    stage_c(0, half, d).start()
                stage_z(half, 0).wait_recv()
                stage_c(1, half, 0).start()

        @pl.when(k == 10)
        def _():
            for half in range(2):
                stage_b(half * 3 + 1).wait_recv()
                stage_z(half, 2).start()
                stage_c(0, half, 2).start()

        @pl.when(k == 14)
        def _():
            for half in range(2):
                for d in (1, 3):
                    stage_z(half, d).wait_recv()
                    stage_c(1, half, d).start()

        return carry

    def send_block(k):
        dy, dx = gray(3 - k // NX), gray(3 - lax.rem(k, NX))
        return remote(ho.at[k], recv.at[k], h_s.at[k], h_r.at[k], head_dev(dy, dx))

    lax.fori_loop(0, 16, step, 0)
    for half in range(2):
        stage_z(half, 2).wait_recv()
        stage_c(1, half, 2).start()
    for kind in range(2):
        for half in range(2):
            for d in range(4):
                stage_c(kind, half, d).wait_recv()

    def project(g, first, last):
        for i in range(4):
            if 4 * g + i < 15:
                send_block(4 * g + i).wait_recv()
        dy = gray(3 - g)
        yy = at(y, NX - dy)
        xs = [at(x, NX - int(e)) for e in (2, 3, 1, 0)]
        act = jnp.concatenate([recv[4 * g + i] for i in range(4)], axis=1)
        for j in range(4):
            cols = slice(j * 512, (j + 1) * 512)
            wt = jnp.concatenate([w4[yy, xx, :, cols] for xx in xs], axis=0)
            r = jnp.dot(act, wt, preferred_element_type=F32)
            if not first:
                r = oacc[:, cols] + r
            if last:
                o_ref[:, cols] = r.astype(BF16)
                put(j).start()
            else:
                oacc[:, cols] = r

    def put(j):
        cols = pl.ds(j * 512, 512)
        return pltpu.make_async_copy(o_ref.at[:, cols], out_hbm.at[:, cols], osem.at[j])

    for g in range(4):
        project(g, g == 0, g == 3)

    for i in range(6):
        stage_a(i).wait_send()
        stage_b(i).wait_send()
    for half in range(2):
        for d in range(4):
            stage_z(half, d).wait_send()
            stage_c(0, half, d).wait_send()
            stage_c(1, half, d).wait_send()
    for d in range(1, 8):

        @pl.when(s + d < 8)
        def _(d=d):
            prefix_send(d).wait_send()

    def sent(k, carry):
        send_block(k).wait_send()
        return carry

    lax.fori_loop(0, 15, sent, 0)
    for j in range(4):
        put(j).wait()


def per_device(query, keys, values, mem_init, beta, mem_gain, loc_gain, w_out):
    tokens = query.shape[0]
    any_spec = pl.BlockSpec(memory_space=pl.ANY)
    vmem = pl.BlockSpec(memory_space=pltpu.VMEM)
    dma = pltpu.SemaphoreType.DMA
    attn_out, prefix = pl.pallas_call(
        kernel,
        out_shape=(
            jax.ShapeDtypeStruct((BLK, D), BF16),
            jax.ShapeDtypeStruct((1, 1, HD, HD), F32),
        ),
        in_specs=[
            pl.BlockSpec(memory_space=pltpu.SMEM),
            any_spec, any_spec, any_spec, vmem, vmem, vmem, any_spec,
        ],
        out_specs=(any_spec, vmem),
        scratch_shapes=[
            pltpu.VMEM((tokens, HD), BF16),
            pltpu.VMEM((tokens, HD), BF16),
            pltpu.VMEM((tokens, HD), BF16),
            pltpu.VMEM((NSEG, HD, HD), F32),
            pltpu.VMEM((HD, HD), F32),
            pltpu.VMEM((7, HD, HD), F32),
            pltpu.VMEM((HD, HD), F32),
            pltpu.VMEM((NSEG, 2 * HD, HD), BF16),
            pltpu.VMEM((BLK, SEG), F32),
            pltpu.VMEM((BLK, 2 * HD), F32),
            pltpu.VMEM((15, BLK, HD), BF16),
            pltpu.VMEM((16, BLK, HD), BF16),
            pltpu.VMEM((NX, NX, HD, D), BF16),
            pltpu.VMEM((BLK, D), F32),
            pltpu.VMEM((BLK, D), BF16),
            dma((12,)), dma((2,)), dma((4,)),
            dma((6,)), dma((6,)), dma((6,)), dma((6,)), dma((8,)), dma((8,)),
            dma((16,)), dma((16,)), dma((7,)), dma((7,)), dma((15,)), dma((15,)),
        ],
        compiler_params=pltpu.CompilerParams(
            collective_id=0, has_side_effects=True, vmem_limit_bytes=60 * 2**20
        ),
        name="layer",
    )(
        beta, query, keys, values, mem_init,
        mem_gain.reshape(1, HD), loc_gain.reshape(1, HD), w_out,
    )
    return attn_out, prefix


def solution(mesh):
    in_specs = (
        P("seq", "head"),
        P("seq", "head"),
        P("seq", "head"),
        P("head", None, None),
        P("head"),
        P("head"),
        P("head"),
        P("head", None),
    )
    out_specs = (P(("seq", "head"), None), P("seq", "head", None, None))
    return jax.shard_map(
        per_device, mesh=mesh, in_specs=in_specs, out_specs=out_specs, check_vma=False
    )
```

profile of v0, /device:TPU:91, one launch (start us, length us, event | category | flops | bytes accessed | tf_op | source)
XLA Modules:
  0.0 69.3 jit_solution(7938227194660485764)
XLA Ops:
  1.3 64.2 %layer.1 = (bf16[512,2048]{1,0:T(8,128)(2,1)}, f32[1,1,128,128]{3,2,1,0:T(8,128)}) custom-call(f32[1]{0:T(128)S(6)} %copy.12.beta_ref, bf16[8192,128]{1,0:T(8,128)(2,1)} %q_hbm.1, bf16[8192,128]{1,0:T(8,128)(2,1)} %k_hbm.1, bf16[8192,128]{1,0:T(8,128)(2,1)} %v_hbm.1, f32[1,128,128]{2,1,0:T(8,128)} %init_ref.1, f32[1,128]{1,0:T(1,128)} %bitcast.2, ...), custom_call_target="tpu_custom_call" | custom-call | tf_op jit(solution)/shard_map/layer/pallas_call | solution.py:368
  65.5 0.0 copy-start
  65.5 3.2 %copy.13 = bf16[512,2048]{1,0:T(8,128)(2,1)} copy(bf16[512,2048]{1,0:T(8,128)(2,1)} %get-tuple-element.4) | data formatting | bytes 4194304
  68.7 0.0 copy-done
  68.7 0.6 copy.14
Async XLA Ops:
  65.5 3.2 %copy-start = (f32[1,1,128,128]{3,2,1,0:T(8,128)S(1)}, f32[1,1,128,128]{3,2,1,0:T(8,128)}, u32[]{:S(2)}) copy-start(f32[1,1,128,128]{3,2,1,0:T(8,128)} %get-tuple-element.5) | copy-start | bytes 196612
where the time goes:
time: 69.5 us; the launch traced here: 69.3 us
  Pallas kernels  64.2 us (92%)
  local copies, waits for them, and re-layouts  3.82 us (5%)
  between operations  1.29 us (2%)
    pallas_call x1, Pallas kernels, per_device(): pl.pallas_call(kernel, out_shape=(jax.ShapeDtypeStruct((BLK, D), BF16), j...  64.2 us
    unnamed x4, local copies, waits for them, and re-layouts  3.82 us

commit v1 on v0

v1 whole, which is shorter than its diff:
```python
import functools
import math

import jax
import jax.numpy as jnp
from jax import lax
from jax.experimental import pallas as pl
from jax.experimental.pallas import tpu as pltpu
from jax.sharding import PartitionSpec as P

HD = 128
SEG = 2048
BLK = 512
D = 2048
NSEG = 4
NX = 4
WS = 256
EPS = 1e-06
MESH = pl.DeviceIdType.MESH
F32 = jnp.float32
BF16 = jnp.bfloat16
C2 = HD**-0.5 * math.log2(math.e)


def attend(b, base, q_ref, k_ref, v_ref, s_ref, acc_ref):
    half = BLK // 2
    q = q_ref[pl.ds(pl.multiple_of(base + b * BLK, BLK), BLK), :]

    def score(row0, rows, key0, cols, masked):
        k = k_ref[pl.ds(pl.multiple_of(base + key0, 256), cols), :]
        s = lax.dot_general(
            q[row0 : row0 + rows], k, (((1,), (1,)), ((), ())), preferred_element_type=F32
        )
        s = s * C2
        if masked:
            col = lax.broadcasted_iota(jnp.int32, (rows, cols), 1) + (key0 - b * BLK)
            row = lax.broadcasted_iota(jnp.int32, (rows, cols), 0) + row0
            s = jnp.where(col <= row, s, -jnp.inf)
        s_ref[row0 : row0 + rows, key0 : key0 + cols] = s
        top = s[:, 0:128]
        for t in range(1, cols // 128):
            top = jnp.maximum(top, s[:, t * 128 : (t + 1) * 128])
        return top

    tops = [None, None]

    def merge(i, top):
        tops[i] = top if tops[i] is None else jnp.maximum(tops[i], top)

    for key0 in range(0, b * BLK, BLK):
        top = score(0, BLK, key0, BLK, False)
        merge(0, top[:half])
        merge(1, top[half:])
    merge(1, score(half, half, b * BLK, half, False))
    merge(0, score(0, half, b * BLK, half, True))
    merge(1, score(half, half, b * BLK + half, half, True))
    for i in range(2):
        largest = jnp.max(tops[i], axis=1, keepdims=True)
        length = b * BLK + (i + 1) * half
        rows = slice(i * half, (i + 1) * half)
        p = jnp.exp2(s_ref[rows, 0:length] - largest).astype(BF16)
        v = v_ref[pl.ds(pl.multiple_of(base, SEG), length), :]
        v = jnp.concatenate([v, jnp.ones((length, HD), BF16)], axis=1)
        acc_ref[rows, :] = jnp.dot(p, v, preferred_element_type=F32)


def feature(x):
    x = x.astype(F32)
    return jnp.where(x > 0, x + 1.0, jnp.exp(x)).astype(BF16)


ORDER = (
    (2, 2), (1, 1), (3, 3), (3, 1), (1, 3), (1, 2), (2, 1), (3, 2),
    (2, 3), (1, 0), (3, 0), (2, 0), (0, 1), (0, 3), (0, 2), (0, 0),
)
HOLD = 4
SERVICE = {
    1: (("own", 3),),
    3: (("own", 4),),
    4: (("own", 5), ("z", 0), ("z", 1), ("z", 2)),
    7: (("z", 3),),
    11: (("z", 4),),
    14: (("z", 5),),
}


def pick(k, table):
    if isinstance(k, int):
        return table[k]
    value = jnp.int32(table[0])
    for i in range(1, len(table)):
        value = jnp.where(k == i, jnp.int32(table[i]), value)
    return value


def kernel(
    beta_ref, q_hbm, k_hbm, v_hbm, init_hbm, mg_hbm, lg_hbm, w_hbm,
    out_ref, prefix_ref,
    q_ref, k_ref, v_ref, kv_ref, tot_ref, trecv, base_ref, memcat, s_ref, acc_ref,
    ho, recv, w8, oacc,
    init_ref, mg_ref, lg_ref, lsem, wsem, psem,
    a_s, a_r, z_s, z_r, r_s, r_r, c_s, c_r, t_s, t_r, h_s, h_r,
):
    s = lax.axis_index("seq")
    h = lax.axis_index("head")
    z, c = s // 2, lax.rem(s, 2)
    y, x = h // NX, lax.rem(h, NX)

    def at(v, d):
        return lax.rem(v + d, NX)

    def head_dev(dy, dx):
        return (s, at(y, dy) * NX + at(x, dx))

    def z_dev(d):
        return (at(z, d) * 2 + c, h)

    mate = (z * 2 + (1 - c), h)

    def remote(src, dst, ssem, rsem, dev):
        return pltpu.make_async_remote_copy(
            src_ref=src, dst_ref=dst, send_sem=ssem, recv_sem=rsem,
            device_id=dev, device_id_type=MESH,
        )

    barrier = pltpu.get_barrier_semaphore()

    def greet_head(i, carry):
        pl.semaphore_signal(
            barrier, inc=1, device_id=(s, lax.rem(h + i, 16)), device_id_type=MESH
        )
        return carry

    lax.fori_loop(1, 16, greet_head, 0)

    def greet_seq(i, carry):
        pl.semaphore_signal(
            barrier, inc=1, device_id=(lax.rem(s + i, 8), h), device_id_type=MESH
        )
        return carry

    lax.fori_loop(1, 8, greet_seq, 0)

    def load(which, n):
        src = (k_hbm, v_hbm, q_hbm)[which]
        dst = (k_ref, v_ref, q_ref)[which]
        span = pl.ds(n * SEG, SEG)
        return pltpu.make_async_copy(src.at[span], dst.at[span], lsem.at[which * NSEG + n])

    def slice_of(dz):
        return at(z, dz) * 2 + c

    def own(i):
        sl = lax.rem(slice_of(0) + i, 8)
        return pltpu.make_async_copy(
            w_hbm.at[:, pl.ds(pl.multiple_of(sl * WS, WS), WS)], w8.at[sl, y, x], wsem.at[i]
        )

    own(0).start()
    for n in range(NSEG):
        load(0, n).start()
        load(1, n).start()

    def stage_a(dy, dx):
        ref = w8.at[slice_of(0), y, x]
        i = dy * NX + dx
        return remote(ref, ref, a_s.at[i], a_r.at[i], head_dev(dy, dx))

    PIECES = ((0, 1), (0, 3), (0, 2), (1, None), (3, None), (2, None))

    def piece(dz, p):
        dy, dx = PIECES[p]
        if dx is None:
            return w8.at[slice_of(dz), at(y, NX - dy)]
        return w8.at[slice_of(dz), y, at(x, NX - dx)]

    def stage_z(p, way):
        ref = piece(0, p)
        return remote(
            ref, ref, z_s.at[p * 2 + way], z_r.at[p * 2 + way], z_dev(1 if way == 0 else 3)
        )

    def upward(p):
        return PIECES[p][0] in (0, 3)

    def stage_r(p):
        ref = piece(3 if upward(p) else 1, p)
        return remote(ref, ref, r_s.at[p], r_r.at[p], z_dev(1 if upward(p) else 3))

    def stage_c(dz, p):
        ref = piece(dz, p)
        return remote(ref, ref, c_s.at[dz * 6 + p], c_r.at[dz * 6 + p], mate)

    def forward_own(p):
        dy, dx = PIECES[p]
        for d in range(NX) if dx is None else (dx,):
            stage_a(dy, d).wait_recv()
        stage_z(p, 0).start()
        stage_z(p, 1).start()
        stage_c(0, p).start()

    def forward_z(p):
        stage_z(p, 0).wait_recv()
        if upward(p):
            stage_r(p).start()
        stage_c(3, p).start()
        stage_z(p, 1).wait_recv()
        if not upward(p):
            stage_r(p).start()
        stage_c(1, p).start()

    def forward_r(p):
        stage_r(p).wait_recv()
        stage_c(2, p).start()

    def prefix_send(d):
        return remote(
            tot_ref, trecv.at[d - 1], t_s.at[d - 1], t_r.at[d - 1], (lax.rem(s + d, 8), h)
        )

    def kv_term(n):
        load(0, n).wait()
        load(1, n).wait()
        span = slice(n * SEG, (n + 1) * SEG)
        kv_ref[n] = lax.dot_general(
            feature(k_ref[span, :]), v_ref[span, :], (((0,), (0,)), ((), ())),
            preferred_element_type=F32,
        )

    own(0).wait()
    pl.semaphore_wait(barrier, 22)
    for dy in (0, 1, 3, 2):
        for dx in (1, 3, 0, 2):
            if dy or dx:
                stage_a(dy, dx).start()
    for n in range(NSEG):
        load(2, n).start()
    for i in range(1, 8):
        own(i).start()
    small = [
        pltpu.make_async_copy(src, dst, psem.at[i])
        for i, (src, dst) in enumerate(
            ((init_hbm, init_ref), (mg_hbm, mg_ref), (lg_hbm, lg_ref))
        )
    ]
    for copy in small:
        copy.start()
    for n in range(NSEG):
        kv_term(n)
    tot_ref[...] = (kv_ref[0] + kv_ref[1]) + (kv_ref[2] + kv_ref[3])
    for d in range(1, 8):

        @pl.when(s + d < 8)
        def _(d=d):
            prefix_send(d).start()

    for n in range(NSEG):
        load(2, n).wait()
    for copy in small:
        copy.wait()
    for i in range(1, 8):
        own(i).wait()
    for p in range(3):
        forward_own(p)

    gate = 1.0 / (1.0 + jnp.exp(-jnp.full((1, HD), beta_ref[0], F32)))
    mem_scale = gate * mg_ref[...]
    loc_scale = (1.0 - gate) * lg_ref[...]

    def offsets(k):
        return pick(k, [o[0] for o in ORDER]), pick(k, [o[1] for o in ORDER])

    def send_block(k):
        dy, dx = offsets(k)
        return remote(ho.at[k], recv.at[k], h_s.at[k], h_r.at[k], head_dev(dy, dx))

    def step(k, carry):
        dy, dx = offsets(k)
        n, b = at(y, dy), at(x, dx)
        base = pl.multiple_of(n * SEG, SEG)
        for bb in range(4):

            @pl.when(b == bb)
            def _(bb=bb):
                attend(bb, base, q_ref, k_ref, v_ref, s_ref, acc_ref)

        @pl.when(k == 0)
        def _():
            base_ref[...] = init_ref[0]
            for d in range(1, 8):

                @pl.when(s - d >= 0)
                def _(d=d):
                    prefix_send(d).wait_recv()
                    base_ref[...] += trecv[d - 1]

            running = base_ref[...]
            prefix_ref[0, 0] = running * (NSEG * SEG) ** -0.5
            for m in range(NSEG):
                top = running.astype(BF16)
                memcat[m, 0:HD, :] = top
                memcat[m, HD : 2 * HD, :] = (running - top.astype(F32)).astype(BF16)
                if m < NSEG - 1:
                    running = running + kv_ref[m]

        feat = feature(q_ref[pl.ds(pl.multiple_of(base + b * BLK, BLK), BLK), :])
        read = jnp.dot(
            jnp.concatenate([feat, feat], axis=1), memcat[n], preferred_element_type=F32
        )
        read_sq = jnp.mean(read * read, axis=-1, keepdims=True)
        total = acc_ref[:, 0:HD]
        weight = acc_ref[:, HD : HD + 1]
        total_sq = jnp.mean(total * total, axis=-1, keepdims=True)
        mixed = (read * lax.rsqrt(read_sq + EPS)) * mem_scale + (
            total * lax.rsqrt(total_sq + EPS * (weight * weight))
        ) * loc_scale
        mixed = mixed.astype(BF16)

        @pl.when(k < 15)
        def _():
            ho[k] = mixed

        @pl.when(k == 15)
        def _():
            recv[15] = mixed

        for when, todo in SERVICE.items():

            @pl.when(k == when)
            def _(todo=todo):
                for what, p in todo:
                    (forward_own if what == "own" else forward_z)(p)

        @pl.when(k == HOLD)
        def _():
            def send(i, carry):
                send_block(i).start()
                return carry

            lax.fori_loop(0, HOLD, send, 0)

        @pl.when((k >= HOLD) & (k < 15))
        def _():
            send_block(k).start()

        return carry

    lax.fori_loop(0, 16, step, 0)

    def slice_at(j):
        dz = pick(j // 2, [0, 3, 1, 2])
        return at(z, dz) * 2 + lax.rem(c + j, 2)

    def arrived(g):
        for i in range(4 * g, min(4 * g + 4, 15)):
            send_block(i).wait_recv()

    def project(slots, js, first, last):
        act = jnp.concatenate([recv[i] for i in slots], axis=1)
        for j in js:
            sl = slice_at(j)
            cols = pl.ds(pl.multiple_of(sl * WS, WS), WS)
            wt = [w8[sl, at(y, NX - ORDER[i][0]), at(x, NX - ORDER[i][1])] for i in slots]
            r = jnp.dot(act, jnp.concatenate(wt, axis=0), preferred_element_type=F32)
            if not first:
                r = oacc[:, cols] + r
            if last:
                out_ref[:, cols] = r.astype(BF16)
            else:
                oacc[:, cols] = r

    near, far = range(6), range(6, 8)
    early = [i for i in range(16) if ORDER[i][0] in (0, 1)]
    late = [i for i in range(16) if ORDER[i][0] in (3, 2)]
    for dz in (0, 3, 1):
        for p in range(6):
            stage_c(dz, p).wait_recv()
    arrived(0)
    project(range(0, 4), near, True, False)
    arrived(1)
    project(range(4, 8), near, False, False)
    for p in (0, 1, 2, 3):
        forward_r(p)
    arrived(2)
    project(range(8, 12), near, False, False)
    for p in (4, 5):
        forward_r(p)
    arrived(3)
    project(range(12, 16), near, False, True)
    for p in (0, 1, 2, 3):
        stage_c(2, p).wait_recv()
    project(early, far, True, False)
    for p in (4, 5):
        stage_c(2, p).wait_recv()
    project(late, far, False, True)

    for dy in range(NX):
        for dx in range(NX):
            if dy or dx:
                stage_a(dy, dx).wait_send()
    for p in range(6):
        stage_z(p, 0).wait_send()
        stage_z(p, 1).wait_send()
        stage_r(p).wait_send()
        for dz in range(4):
            stage_c(dz, p).wait_send()
    for d in range(1, 8):

        @pl.when(s + d < 8)
        def _(d=d):
            prefix_send(d).wait_send()

    def sent(k, carry):
        send_block(k).wait_send()
        return carry

    lax.fori_loop(0, 15, sent, 0)


def per_device(query, keys, values, mem_init, beta, mem_gain, loc_gain, w_out):
    tokens = query.shape[0]
    hbm = pl.BlockSpec(memory_space=pltpu.HBM)
    vmem = pl.BlockSpec(memory_space=pltpu.VMEM)
    dma = pltpu.SemaphoreType.DMA
    attn_out, prefix = pl.pallas_call(
        kernel,
        out_shape=(
            pltpu.VMEM((BLK, D), BF16),
            pltpu.VMEM((1, 1, HD, HD), F32),
        ),
        in_specs=[
            pl.BlockSpec(memory_space=pltpu.SMEM),
            hbm, hbm, hbm, hbm, hbm, hbm, hbm,
        ],
        out_specs=(vmem, vmem),
        scratch_shapes=[
            pltpu.VMEM((tokens, HD), BF16),
            pltpu.VMEM((tokens, HD), BF16),
            pltpu.VMEM((tokens, HD), BF16),
            pltpu.VMEM((NSEG, HD, HD), F32),
            pltpu.VMEM((HD, HD), F32),
            pltpu.VMEM((7, HD, HD), F32),
            pltpu.VMEM((HD, HD), F32),
            pltpu.VMEM((NSEG, 2 * HD, HD), BF16),
            pltpu.VMEM((BLK, SEG), F32),
            pltpu.VMEM((BLK, 2 * HD), F32),
            pltpu.VMEM((15, BLK, HD), BF16),
            pltpu.VMEM((16, BLK, HD), BF16),
            pltpu.VMEM((8, NX, NX, HD, WS), BF16),
            pltpu.VMEM((BLK, D), F32),
            pltpu.VMEM((1, HD, HD), F32),
            pltpu.VMEM((1, HD), F32),
            pltpu.VMEM((1, HD), F32),
            dma((12,)), dma((8,)), dma((3,)),
            dma((16,)), dma((16,)), dma((12,)), dma((12,)), dma((6,)), dma((6,)),
            dma((24,)), dma((24,)), dma((7,)), dma((7,)), dma((15,)), dma((15,)),
        ],
        compiler_params=pltpu.CompilerParams(
            collective_id=0, has_side_effects=True, vmem_limit_bytes=52 * 2**20
        ),
        name="layer",
    )(
        beta, query, keys, values, mem_init,
        mem_gain.reshape(1, HD), loc_gain.reshape(1, HD), w_out,
    )
    return attn_out, prefix


def solution(mesh):
    in_specs = (
        P("seq", "head"),
        P("seq", "head"),
        P("seq", "head"),
        P("head", None, None),
        P("head"),
        P("head"),
        P("head"),
        P("head", None),
    )
    out_specs = (P(("seq", "head"), None), P("seq", "head", None, None))
    return jax.shard_map(
        per_device, mesh=mesh, in_specs=in_specs, out_specs=out_specs, check_vma=False
    )
```

time: 69.5 us -> 57.2 us (0.82)
  the two profiles are of different devices: /device:TPU:91 before, /device:TPU:1 now
where the time goes in v1:
time: 57.2 us; the launch traced here: 57.1 us
  Pallas kernels  53.9 us (94%)
  local copies, waits for them, and re-layouts  1.95 us (3%)
  between operations  1.29 us (2%)
    pallas_call x1, Pallas kernels, per_device(): pl.pallas_call(kernel, out_shape=(pltpu.VMEM((BLK, D), BF16), pltpu.VMEM(...  53.9 us
    unnamed x2, local copies, waits for them, and re-layouts  1.95 us

profile of v1, /device:TPU:1, one launch (start us, length us, event | category | flops | bytes accessed | tf_op | source)
XLA Modules:
  0.0 57.1 jit_solution(16532713435921742177)
XLA Ops:
  1.3 53.9 %layer.1 = (bf16[512,2048]{1,0:T(8,128)(2,1)S(1)}, f32[1,1,128,128]{3,2,1,0:T(8,128)S(1)}) custom-call(f32[1]{0:T(128)S(6)} %copy.14.beta_ref, bf16[8192,128]{1,0:T(8,128)(2,1)} %q_hbm.1, bf16[8192,128]{1,0:T(8,128)(2,1)} %k_hbm.1, bf16[8192,128]{1,0:T(8,128)(2,1)} %v_hbm.1, f32[1,128,128]{2,1,0:T(8,128)} %init_hbm.1, f32[1,128]{1,0:T(1,128)} %bitcast.2, ...), custom_call_target="tpu_custom_call" | custom-call | tf_op jit(solution)/shard_map/layer/pallas_call | solution.py:425
  55.1 1.3 %copy.12 = bf16[512,2048]{1,0:T(8,128)(2,1)} copy(bf16[512,2048]{1,0:T(8,128)(2,1)S(1)} %get-tuple-element.2) | data formatting | bytes 4194304
  56.5 0.6 %copy.13 = f32[1,1,128,128]{3,2,1,0:T(8,128)} copy(f32[1,1,128,128]{3,2,1,0:T(8,128)S(1)} %get-tuple-element.3) | data formatting | bytes 131072

commit v2 on v1

--- a/solution.py
+++ b/solution.py
@@ -96,7 +96,7 @@
 def kernel(
     beta_ref, q_hbm, k_hbm, v_hbm, init_hbm, mg_hbm, lg_hbm, w_hbm,
     out_ref, prefix_ref,
-    q_ref, k_ref, v_ref, kv_ref, tot_ref, trecv, base_ref, memcat, s_ref, acc_ref,
+    q_ref, k_ref, v_ref, kv_ref, tot_ref, chip_ref, trecv, base_ref, memcat, s_ref, acc_ref,
     ho, recv, w8, oacc,
     init_ref, mg_ref, lg_ref, lsem, wsem, psem,
     a_s, a_r, z_s, z_r, r_s, r_r, c_s, c_r, t_s, t_r, h_s, h_r,
@@ -133,13 +133,8 @@
 
     lax.fori_loop(1, 16, greet_head, 0)
 
-    def greet_seq(i, carry):
-        pl.semaphore_signal(
-            barrier, inc=1, device_id=(lax.rem(s + i, 8), h), device_id_type=MESH
-        )
-        return carry
-
-    lax.fori_loop(1, 8, greet_seq, 0)
+    for dev in (mate, z_dev(1), z_dev(2), z_dev(3)):
+        pl.semaphore_signal(barrier, inc=1, device_id=dev, device_id_type=MESH)
 
     def load(which, n):
         src = (k_hbm, v_hbm, q_hbm)[which]
@@ -156,15 +151,16 @@
             w_hbm.at[:, pl.ds(pl.multiple_of(sl * WS, WS), WS)], w8.at[sl, y, x], wsem.at[i]
         )
 
-    own(0).start()
     for n in range(NSEG):
         load(0, n).start()
         load(1, n).start()
 
     def stage_a(dy, dx):
-        ref = w8.at[slice_of(0), y, x]
         i = dy * NX + dx
-        return remote(ref, ref, a_s.at[i], a_r.at[i], head_dev(dy, dx))
+        src = w_hbm.at[:, pl.ds(pl.multiple_of(slice_of(0) * WS, WS), WS)]
+        return remote(
+            src, w8.at[slice_of(0), y, x], a_s.at[i], a_r.at[i], head_dev(dy, dx)
+        )
 
     PIECES = ((0, 1), (0, 3), (0, 2), (1, None), (3, None), (2, None))
 
@@ -213,10 +209,11 @@
         stage_r(p).wait_recv()
         stage_c(2, p).start()
 
+    def mate_send():
+        return remote(tot_ref, trecv.at[0], t_s.at[0], t_r.at[0], mate)
+
     def prefix_send(d):
-        return remote(
-            tot_ref, trecv.at[d - 1], t_s.at[d - 1], t_r.at[d - 1], (lax.rem(s + d, 8), h)
-        )
+        return remote(chip_ref, trecv.at[d], t_s.at[d], t_r.at[d], z_dev(d))
 
     def kv_term(n):
         load(0, n).wait()
@@ -227,15 +224,14 @@
             preferred_element_type=F32,
         )
 
-    own(0).wait()
-    pl.semaphore_wait(barrier, 22)
+    pl.semaphore_wait(barrier, 19)
     for dy in (0, 1, 3, 2):
         for dx in (1, 3, 0, 2):
             if dy or dx:
                 stage_a(dy, dx).start()
     for n in range(NSEG):
         load(2, n).start()
-    for i in range(1, 8):
+    for i in range(8):
         own(i).start()
     small = [
         pltpu.make_async_copy(src, dst, psem.at[i])
@@ -248,20 +244,23 @@
     for n in range(NSEG):
         kv_term(n)
     tot_ref[...] = (kv_ref[0] + kv_ref[1]) + (kv_ref[2] + kv_ref[3])
-    for d in range(1, 8):
-
-        @pl.when(s + d < 8)
+    mate_send().start()
+    mate_send().wait_recv()
+    chip_ref[...] = tot_ref[...] + trecv[0]
+    for d in range(1, NX):
+
+        @pl.when(z + d < NX)
         def _(d=d):
             prefix_send(d).start()
 
+    for p in range(3):
+        forward_own(p)
     for n in range(NSEG):
         load(2, n).wait()
     for copy in small:
         copy.wait()
-    for i in range(1, 8):
+    for i in range(8):
         own(i).wait()
-    for p in range(3):
-        forward_own(p)
 
     gate = 1.0 / (1.0 + jnp.exp(-jnp.full((1, HD), beta_ref[0], F32)))
     mem_scale = gate * mg_ref[...]
@@ -287,12 +286,16 @@
         @pl.when(k == 0)
         def _():
             base_ref[...] = init_ref[0]
-            for d in range(1, 8):
-
-                @pl.when(s - d >= 0)
+            for d in range(1, NX):
+
+                @pl.when(z - d >= 0)
                 def _(d=d):
                     prefix_send(d).wait_recv()
-                    base_ref[...] += trecv[d - 1]
+                    base_ref[...] += trecv[d]
+
+            @pl.when(c == 1)
+            def _():
+                base_ref[...] += trecv[0]
 
             running = base_ref[...]
             prefix_ref[0, 0] = running * (NSEG * SEG) ** -0.5
@@ -370,8 +373,9 @@
                 oacc[:, cols] = r
 
     near, far = range(6), range(6, 8)
-    early = [i for i in range(16) if ORDER[i][0] in (0, 1)]
-    late = [i for i in range(16) if ORDER[i][0] in (3, 2)]
+    done = [0, 1, 2, 3, 4, 5, 6, 7, 12, 13, 14, 15]
+    early = [i for i in done if ORDER[i][0] in (0, 1)]
+    late = [i for i in done if ORDER[i][0] in (3, 2)]
     for dz in (0, 3, 1):
         for p in range(6):
             stage_c(dz, p).wait_recv()
@@ -381,18 +385,18 @@
     project(range(4, 8), near, False, False)
     for p in (0, 1, 2, 3):
         forward_r(p)
-    arrived(2)
-    project(range(8, 12), near, False, False)
+    arrived(3)
+    project(range(12, 16), near, False, False)
     for p in (4, 5):
         forward_r(p)
-    arrived(3)
-    project(range(12, 16), near, False, True)
     for p in (0, 1, 2, 3):
         stage_c(2, p).wait_recv()
     project(early, far, True, False)
     for p in (4, 5):
         stage_c(2, p).wait_recv()
-    project(late, far, False, True)
+    project(late, far, False, False)
+    arrived(2)
+    project(range(8, 12), range(8), False, True)
 
     for dy in range(NX):
         for dx in range(NX):
@@ -404,9 +408,10 @@
         stage_r(p).wait_send()
         for dz in range(4):
             stage_c(dz, p).wait_send()
-    for d in range(1, 8):
-
-        @pl.when(s + d < 8)
+    mate_send().wait_send()
+    for d in range(1, NX):
+
+        @pl.when(z + d < NX)
         def _(d=d):
             prefix_send(d).wait_send()
 
@@ -415,6 +420,17 @@
         return carry
 
     lax.fori_loop(0, 15, sent, 0)
+
+
+def finish(a_ref, p_ref, a_out, p_out, sem):
+    copies = [pltpu.make_async_copy(p_ref, p_out, sem.at[4])]
+    for i in range(4):
+        rows = pl.ds(i * 128, 128)
+        copies.append(pltpu.make_async_copy(a_ref.at[rows], a_out.at[rows], sem.at[i]))
+    for copy in copies:
+        copy.start()
+    for copy in copies:
+        copy.wait()
 
 
 def per_device(query, keys, values, mem_init, beta, mem_gain, loc_gain, w_out):
@@ -439,7 +455,8 @@
             pltpu.VMEM((tokens, HD), BF16),
             pltpu.VMEM((NSEG, HD, HD), F32),
             pltpu.VMEM((HD, HD), F32),
-            pltpu.VMEM((7, HD, HD), F32),
+            pltpu.VMEM((HD, HD), F32),
+            pltpu.VMEM((NX, HD, HD), F32),
             pltpu.VMEM((HD, HD), F32),
             pltpu.VMEM((NSEG, 2 * HD, HD), BF16),
             pltpu.VMEM((BLK, SEG), F32),
@@ -453,7 +470,7 @@
             pltpu.VMEM((1, HD), F32),
             dma((12,)), dma((8,)), dma((3,)),
             dma((16,)), dma((16,)), dma((12,)), dma((12,)), dma((6,)), dma((6,)),
-            dma((24,)), dma((24,)), dma((7,)), dma((7,)), dma((15,)), dma((15,)),
+            dma((24,)), dma((24,)), dma((4,)), dma((4,)), dma((15,)), dma((15,)),
         ],
         compiler_params=pltpu.CompilerParams(
             collective_id=0, has_side_effects=True, vmem_limit_bytes=52 * 2**20
@@ -463,7 +480,20 @@
         beta, query, keys, values, mem_init,
         mem_gain.reshape(1, HD), loc_gain.reshape(1, HD), w_out,
     )
-    return attn_out, prefix
+    return pl.pallas_call(
+        finish,
+        out_shape=(
+            jax.ShapeDtypeStruct((BLK, D), BF16),
+            jax.ShapeDtypeStruct((1, 1, HD, HD), F32),
+        ),
+        in_specs=[vmem, vmem],
+        out_specs=(hbm, hbm),
+        scratch_shapes=[dma((5,))],
+        name="finish",
+    )(
+        pltpu.with_memory_space_constraint(attn_out, pltpu.VMEM),
+        pltpu.with_memory_space_constraint(prefix, pltpu.VMEM),
+    )
 
 
 def solution(mesh):

time: 57.2 us -> 56.1 us (0.981)
  local copies, waits for them, and re-layouts: 1.95 us -> 0 us
  Pallas kernels: 53.9 us -> 54.5 us
    unnamed x2 -> x0, local copies, waits for them, and re-layouts: 1.95 us -> none
    pallas_call x0 -> x1, Pallas kernels: none -> 1.38 us  [per_device(): pl.pallas_call(finish, out_shape=(jax.ShapeDtypeStruct((BLK, D), BF16), j...]
    pallas_call x1, Pallas kernels: 53.9 us -> 53.2 us  [per_device(): pl.pallas_call(kernel, out_shape=(pltpu.VMEM((BLK, D), BF16), pltpu.VMEM(...]
where the time goes in v2:
time: 56.1 us; the launch traced here: 55.8 us
  Pallas kernels  54.5 us (97%)
  between operations  1.29 us (2%)
    pallas_call x1, Pallas kernels, per_device(): pl.pallas_call(kernel, out_shape=(pltpu.VMEM((BLK, D), BF16), pltpu.VMEM(...  53.2 us
    pallas_call x1, Pallas kernels, per_device(): pl.pallas_call(finish, out_shape=(jax.ShapeDtypeStruct((BLK, D), BF16), j...  1.38 us

profile of v2, /device:TPU:1, one launch (start us, length us, event | category | flops | bytes accessed | tf_op | source)
XLA Modules:
  0.0 55.8 jit_solution(4386134792778743392)
XLA Ops:
  1.3 53.2 %layer.1 = (bf16[512,2048]{1,0:T(8,128)(2,1)S(1)}, f32[1,1,128,128]{3,2,1,0:T(8,128)S(1)}) custom-call(f32[1]{0:T(128)S(6)} %copy.10.beta_ref, bf16[8192,128]{1,0:T(8,128)(2,1)} %q_hbm.1, bf16[8192,128]{1,0:T(8,128)(2,1)} %k_hbm.1, bf16[8192,128]{1,0:T(8,128)(2,1)} %v_hbm.1, f32[1,128,128]{2,1,0:T(8,128)} %init_hbm.1, f32[1,128]{1,0:T(1,128)} %bitcast.2, ...), custom_call_target="tpu_custom_call" | custom-call | tf_op jit(solution)/shard_map/layer/pallas_call | solution.py:441
  54.4 1.4 %finish.1 = (bf16[512,2048]{1,0:T(8,128)(2,1)}, f32[1,1,128,128]{3,2,1,0:T(8,128)}) custom-call(bf16[512,2048]{1,0:T(8,128)(2,1)S(1)} %get-tuple-element.4.a_ref, f32[1,1,128,128]{3,2,1,0:T(8,128)S(1)} %get-tuple-element.5.p_ref), custom_call_target="tpu_custom_call" | custom-call | tf_op jit(solution)/shard_map/finish/pallas_call | solution.py:483

commit v3 on v2

--- a/solution.py
+++ b/solution.py
@@ -73,14 +73,22 @@
     (2, 2), (1, 1), (3, 3), (3, 1), (1, 3), (1, 2), (2, 1), (3, 2),
     (2, 3), (1, 0), (3, 0), (2, 0), (0, 1), (0, 3), (0, 2), (0, 0),
 )
-HOLD = 4
+HOLD = 3
+LAST = (8, 9, 10, 11)
+NEAR = ((0, 1), (0, 3), (1, 0), (3, 0))
+NEAR_PIECE = (0, 1, 3, 4)
+RELAY = (
+    (2, 0, 2, True),
+    (3, 1, 1, False), (3, 1, 3, False), (3, 1, 2, False),
+    (4, 3, 1, True), (4, 3, 3, True), (4, 3, 2, True),
+    (5, 2, 0, True), (5, 2, 1, True), (5, 2, 2, False), (5, 2, 3, False),
+)
 SERVICE = {
-    1: (("own", 3),),
-    3: (("own", 4),),
-    4: (("own", 5), ("z", 0), ("z", 1), ("z", 2)),
-    7: (("z", 3),),
-    11: (("z", 4),),
-    14: (("z", 5),),
+    1: (("own", 4),),
+    3: (("own", 5), ("z", 0), ("z", 1), ("z", 2)),
+    6: (("z", 3),),
+    10: (("z", 4),),
+    13: (("z", 5),),
 }
 
 
@@ -94,12 +102,11 @@
 
 
 def kernel(
-    beta_ref, q_hbm, k_hbm, v_hbm, init_hbm, mg_hbm, lg_hbm, w_hbm,
-    out_ref, prefix_ref,
+    beta_hbm, q_hbm, k_hbm, v_hbm, init_hbm, mg_hbm, lg_hbm, w_hbm,
+    oacc, recv, w8, prefix_ref,
     q_ref, k_ref, v_ref, kv_ref, tot_ref, chip_ref, trecv, base_ref, memcat, s_ref, acc_ref,
-    ho, recv, w8, oacc,
-    init_ref, mg_ref, lg_ref, lsem, wsem, psem,
-    a_s, a_r, z_s, z_r, r_s, r_r, c_s, c_r, t_s, t_r, h_s, h_r,
+    ho, beta_ref, init_ref, mg_ref, lg_ref, lsem, wsem, psem,
+    a_s, a_r, z_s, z_r, r_s, r_r, e_s, e_r, c_s, c_r, t_s, t_r, h_s, h_r,
 ):
     s = lax.axis_index("seq")
     h = lax.axis_index("head")
@@ -176,12 +183,16 @@
             ref, ref, z_s.at[p * 2 + way], z_r.at[p * 2 + way], z_dev(1 if way == 0 else 3)
         )
 
-    def upward(p):
-        return PIECES[p][0] in (0, 3)
-
-    def stage_r(p):
-        ref = piece(3 if upward(p) else 1, p)
-        return remote(ref, ref, r_s.at[p], r_r.at[p], z_dev(1 if upward(p) else 3))
+    def stage_e(i):
+        dy, dx = NEAR[i]
+        sl = slice_of(2)
+        src = w_hbm.at[:, pl.ds(pl.multiple_of(sl * WS, WS), WS)]
+        return remote(src, w8.at[sl, y, x], e_s.at[i], e_r.at[i], head_dev(dy, dx))
+
+    def stage_r(i):
+        _, dy, dx, up = RELAY[i]
+        ref = w8.at[slice_of(3 if up else 1), at(y, NX - dy), at(x, NX - dx)]
+        return remote(ref, ref, r_s.at[i], r_r.at[i], z_dev(1 if up else 3))
 
     def stage_c(dz, p):
         ref = piece(dz, p)
@@ -196,17 +207,19 @@
         stage_c(0, p).start()
 
     def forward_z(p):
-        stage_z(p, 0).wait_recv()
-        if upward(p):
-            stage_r(p).start()
-        stage_c(3, p).start()
-        stage_z(p, 1).wait_recv()
-        if not upward(p):
-            stage_r(p).start()
-        stage_c(1, p).start()
+        for way in range(2):
+            stage_z(p, way).wait_recv()
+            for i, (piece_of, _, _, up) in enumerate(RELAY):
+                if piece_of == p and up == (way == 0):
+                    stage_r(i).start()
+            stage_c(3 if way == 0 else 1, p).start()
 
     def forward_r(p):
-        stage_r(p).wait_recv()
+        if p in NEAR_PIECE:
+            stage_e(NEAR_PIECE.index(p)).wait_recv()
+        for i, relay in enumerate(RELAY):
+            if relay[0] == p:
+                stage_r(i).wait_recv()
         stage_c(2, p).start()
 
     def mate_send():
@@ -229,6 +242,8 @@
         for dx in (1, 3, 0, 2):
             if dy or dx:
                 stage_a(dy, dx).start()
+    for i in range(4):
+        stage_e(i).start()
     for n in range(NSEG):
         load(2, n).start()
     for i in range(8):
@@ -236,7 +251,7 @@
     small = [
         pltpu.make_async_copy(src, dst, psem.at[i])
         for i, (src, dst) in enumerate(
-            ((init_hbm, init_ref), (mg_hbm, mg_ref), (lg_hbm, lg_ref))
+            ((init_hbm, init_ref), (mg_hbm, mg_ref), (lg_hbm, lg_ref), (beta_hbm, beta_ref))
         )
     ]
     for copy in small:
@@ -285,6 +300,7 @@
 
         @pl.when(k == 0)
         def _():
+            forward_own(3)
             base_ref[...] = init_ref[0]
             for d in range(1, NX):
 
@@ -354,11 +370,11 @@
         dz = pick(j // 2, [0, 3, 1, 2])
         return at(z, dz) * 2 + lax.rem(c + j, 2)
 
-    def arrived(g):
-        for i in range(4 * g, min(4 * g + 4, 15)):
+    def arrived(slots):
+        for i in slots:
             send_block(i).wait_recv()
 
-    def project(slots, js, first, last):
+    def project(slots, js, first):
         act = jnp.concatenate([recv[i] for i in slots], axis=1)
         for j in js:
             sl = slice_at(j)
@@ -367,36 +383,35 @@
             r = jnp.dot(act, jnp.concatenate(wt, axis=0), preferred_element_type=F32)
             if not first:
                 r = oacc[:, cols] + r
-            if last:
-                out_ref[:, cols] = r.astype(BF16)
-            else:
-                oacc[:, cols] = r
+            oacc[:, cols] = r
 
     near, far = range(6), range(6, 8)
-    done = [0, 1, 2, 3, 4, 5, 6, 7, 12, 13, 14, 15]
+    done = [i for i in range(16) if i not in LAST]
     early = [i for i in done if ORDER[i][0] in (0, 1)]
-    late = [i for i in done if ORDER[i][0] in (3, 2)]
-    for dz in (0, 3, 1):
+    late = [i for i in done if i not in early]
+    for p in range(6):
+        stage_c(0, p).wait_recv()
+    arrived(range(0, 4))
+    project(range(0, 4), (0, 1, 2, 4), True)
+    for p in (0, 1, 2, 3):
+        forward_r(p)
+    arrived(range(4, 8))
+    project(range(4, 8), (0, 1, 2, 4), False)
+    for dz in (3, 1):
         for p in range(6):
             stage_c(dz, p).wait_recv()
-    arrived(0)
-    project(range(0, 4), near, True, False)
-    arrived(1)
-    project(range(4, 8), near, False, False)
-    for p in (0, 1, 2, 3):
-        forward_r(p)
-    arrived(3)
-    project(range(12, 16), near, False, False)
+    project(range(0, 8), (3, 5), True)
     for p in (4, 5):
         forward_r(p)
+    arrived(range(12, 15))
+    project(range(12, 16), near, False)
     for p in (0, 1, 2, 3):
         stage_c(2, p).wait_recv()
-    project(early, far, True, False)
+    project(early, far, True)
     for p in (4, 5):
         stage_c(2, p).wait_recv()
-    project(late, far, False, False)
-    arrived(2)
-    project(range(8, 12), range(8), False, True)
+    project(late, far, False)
+    arrived(LAST)
 
     for dy in range(NX):
         for dx in range(NX):
@@ -405,9 +420,12 @@
     for p in range(6):
         stage_z(p, 0).wait_send()
         stage_z(p, 1).wait_send()
-        stage_r(p).wait_send()
         for dz in range(4):
             stage_c(dz, p).wait_send()
+    for i in range(4):
+        stage_e(i).wait_send()
+    for i in range(len(RELAY)):
+        stage_r(i).wait_send()
     mate_send().wait_send()
     for d in range(1, NX):
 
@@ -422,13 +440,22 @@
     lax.fori_loop(0, 15, sent, 0)
 
 
-def finish(a_ref, p_ref, a_out, p_out, sem):
-    copies = [pltpu.make_async_copy(p_ref, p_out, sem.at[4])]
-    for i in range(4):
-        rows = pl.ds(i * 128, 128)
-        copies.append(pltpu.make_async_copy(a_ref.at[rows], a_out.at[rows], sem.at[i]))
-    for copy in copies:
-        copy.start()
+def finish(acc_ref, recv_ref, w_ref, p_ref, a_out, p_out, o_ref, sem):
+    copies = [pltpu.make_async_copy(p_ref, p_out, sem.at[8])]
+    copies[0].start()
+    h = lax.axis_index("head")
+    y, x = h // NX, lax.rem(h, NX)
+    act = jnp.concatenate([recv_ref[i] for i in LAST], axis=1)
+    for sl in range(8):
+        cols = pl.ds(sl * WS, WS)
+        wt = [
+            w_ref[sl, lax.rem(y + NX - ORDER[i][0], NX), lax.rem(x + NX - ORDER[i][1], NX)]
+            for i in LAST
+        ]
+        r = jnp.dot(act, jnp.concatenate(wt, axis=0), preferred_element_type=F32)
+        o_ref[:, cols] = (acc_ref[:, cols] + r).astype(BF16)
+        copies.append(pltpu.make_async_copy(o_ref.at[:, cols], a_out.at[:, cols], sem.at[sl]))
+        copies[-1].start()
     for copy in copies:
         copy.wait()
 
@@ -438,17 +465,18 @@
     hbm = pl.BlockSpec(memory_space=pltpu.HBM)
     vmem = pl.BlockSpec(memory_space=pltpu.VMEM)
     dma = pltpu.SemaphoreType.DMA
-    attn_out, prefix = pl.pallas_call(
+    kept = pl.pallas_call(
         kernel,
         out_shape=(
-            pltpu.VMEM((BLK, D), BF16),
+            pltpu.VMEM((BLK, D), F32),
+            pltpu.VMEM((16, BLK, HD), BF16),
+            pltpu.VMEM((8, NX, NX, HD, WS), BF16),
             pltpu.VMEM((1, 1, HD, HD), F32),
         ),
         in_specs=[
-            pl.BlockSpec(memory_space=pltpu.SMEM),
-            hbm, hbm, hbm, hbm, hbm, hbm, hbm,
+            hbm, hbm, hbm, hbm, hbm, hbm, hbm, hbm,
         ],
-        out_specs=(vmem, vmem),
+        out_specs=(vmem,) * 4,
         scratch_shapes=[
             pltpu.VMEM((tokens, HD), BF16),
             pltpu.VMEM((tokens, HD), BF16),
@@ -462,18 +490,17 @@
             pltpu.VMEM((BLK, SEG), F32),
             pltpu.VMEM((BLK, 2 * HD), F32),
             pltpu.VMEM((15, BLK, HD), BF16),
-            pltpu.VMEM((16, BLK, HD), BF16),
-            pltpu.VMEM((8, NX, NX, HD, WS), BF16),
-            pltpu.VMEM((BLK, D), F32),
+            pltpu.SMEM((1,), F32),
             pltpu.VMEM((1, HD, HD), F32),
             pltpu.VMEM((1, HD), F32),
             pltpu.VMEM((1, HD), F32),
-            dma((12,)), dma((8,)), dma((3,)),
-            dma((16,)), dma((16,)), dma((12,)), dma((12,)), dma((6,)), dma((6,)),
+            dma((12,)), dma((8,)), dma((4,)),
+            dma((16,)), dma((16,)), dma((12,)), dma((12,)), dma((11,)), dma((11,)),
+            dma((4,)), dma((4,)),
             dma((24,)), dma((24,)), dma((4,)), dma((4,)), dma((15,)), dma((15,)),
         ],
         compiler_params=pltpu.CompilerParams(
-            collective_id=0, has_side_effects=True, vmem_limit_bytes=52 * 2**20
+            collective_id=0, has_side_effects=True, vmem_limit_bytes=40 * 2**20
         ),
         name="layer",
     )(
@@ -486,14 +513,12 @@
             jax.ShapeDtypeStruct((BLK, D), BF16),
             jax.ShapeDtypeStruct((1, 1, HD, HD), F32),
         ),
-        in_specs=[vmem, vmem],
+        in_specs=[vmem] * 4,
         out_specs=(hbm, hbm),
-        scratch_shapes=[dma((5,))],
+        scratch_shapes=[pltpu.VMEM((BLK, D), BF16), dma((9,))],
+        compiler_params=pltpu.CompilerParams(vmem_limit_bytes=16 * 2**20),
         name="finish",
-    )(
-        pltpu.with_memory_space_constraint(attn_out, pltpu.VMEM),
-        pltpu.with_memory_space_constraint(prefix, pltpu.VMEM),
-    )
+    )(*[pltpu.with_memory_space_constraint(part, pltpu.VMEM) for part in kept])
 
 
 def solution(mesh):

time: 56.1 us -> 54.6 us (0.973)
  Pallas kernels: 54.5 us -> 52.9 us
    pallas_call x1, Pallas kernels: 53.2 us -> 50.6 us  [per_device(): pl.pallas_call(kernel, out_shape=(pltpu.VMEM((BLK, D), F32), pltpu.VMEM((...]
    pallas_call x1, Pallas kernels: 1.38 us -> 2.31 us  [per_device(): pl.pallas_call(finish, out_shape=(jax.ShapeDtypeStruct((BLK, D), BF16), j...]
where the time goes in v3:
time: 54.6 us; the launch traced here: 54.2 us
  Pallas kernels  52.9 us (97%)
  between operations  1.29 us (2%)
    pallas_call x1, Pallas kernels, per_device(): pl.pallas_call(kernel, out_shape=(pltpu.VMEM((BLK, D), F32), pltpu.VMEM((...  50.6 us
    pallas_call x1, Pallas kernels, per_device(): pl.pallas_call(finish, out_shape=(jax.ShapeDtypeStruct((BLK, D), BF16), j...  2.31 us

profile of v3, /device:TPU:1, one launch (start us, length us, event | category | flops | bytes accessed | tf_op | source)
XLA Modules:
  0.0 54.2 jit_solution(18145893877232333048)
XLA Ops:
  1.3 50.6 %layer.1 = (f32[512,2048]{1,0:T(8,128)S(1)}, bf16[16,512,128]{2,1,0:T(8,128)(2,1)S(1)}, bf16[8,4,4,128,256]{4,3,2,1,0:T(8,128)(2,1)S(1)}, f32[1,1,128,128]{3,2,1,0:T(8,128)S(1)}) custom-call(f32[1]{0:T(128)S(6)} %copy.10.beta_hbm, bf16[8192,128]{1,0:T(8,128)(2,1)} %q_hbm.1, bf16[8192,128]{1,0:T(8,128)(2,1)} %k_hbm.1, bf16[8192,128]{1,0:T(8,128)(2,1)} %v_hbm.1, ...), custom_call_target="tpu_custom_call" | custom-call | tf_op jit(solution)/shard_map/layer/pallas_call | solution.py:468
  51.9 2.3 %finish.1 = (bf16[512,2048]{1,0:T(8,128)(2,1)}, f32[1,1,128,128]{3,2,1,0:T(8,128)}) custom-call(f32[512,2048]{1,0:T(8,128)S(1)} %get-tuple-element.6.acc_ref, bf16[16,512,128]{2,1,0:T(8,128)(2,1)S(1)} %get-tuple-element.7.recv_ref, bf16[8,4,4,128,256]{4,3,2,1,0:T(8,128)(2,1)S(1)} %get-tuple-element.8.w_ref, f32[1,1,128,128]{3,2,1,0:T(8,128)S(1)} %get-tuple-element.9.p_ref), custom_call_target="tpu_custom_call" | custom-call | tf_op jit(solution)/shard_map/finish/pallas_call | solution.py:510

commit v4 on v3

--- a/solution.py
+++ b/solution.py
@@ -73,7 +73,7 @@
     (2, 2), (1, 1), (3, 3), (3, 1), (1, 3), (1, 2), (2, 1), (3, 2),
     (2, 3), (1, 0), (3, 0), (2, 0), (0, 1), (0, 3), (0, 2), (0, 0),
 )
-HOLD = 3
+HOLD = 2
 LAST = (8, 9, 10, 11)
 NEAR = ((0, 1), (0, 3), (1, 0), (3, 0))
 NEAR_PIECE = (0, 1, 3, 4)

time: 54.6 us -> 53.9 us (0.987)
  no operation moved by 1% of the time
where the time goes in v4:
time: 53.9 us; the launch traced here: 53.8 us
  Pallas kernels  52.5 us (97%)
  between operations  1.29 us (2%)
    pallas_call x1, Pallas kernels, per_device(): pl.pallas_call(kernel, out_shape=(pltpu.VMEM((BLK, D), F32), pltpu.VMEM((...  50.2 us
    pallas_call x1, Pallas kernels, per_device(): pl.pallas_call(finish, out_shape=(jax.ShapeDtypeStruct((BLK, D), BF16), j...  2.31 us

profile of v4, /device:TPU:1, one launch (start us, length us, event | category | flops | bytes accessed | tf_op | source)
XLA Modules:
  0.0 53.8 jit_solution(17265616049620729712)
XLA Ops:
  1.3 50.2 %layer.1 = (f32[512,2048]{1,0:T(8,128)S(1)}, bf16[16,512,128]{2,1,0:T(8,128)(2,1)S(1)}, bf16[8,4,4,128,256]{4,3,2,1,0:T(8,128)(2,1)S(1)}, f32[1,1,128,128]{3,2,1,0:T(8,128)S(1)}) custom-call(f32[1]{0:T(128)S(6)} %copy.10.beta_hbm, bf16[8192,128]{1,0:T(8,128)(2,1)} %q_hbm.1, bf16[8192,128]{1,0:T(8,128)(2,1)} %k_hbm.1, bf16[8192,128]{1,0:T(8,128)(2,1)} %v_hbm.1, ...), custom_call_target="tpu_custom_call" | custom-call | tf_op jit(solution)/shard_map/layer/pallas_call | solution.py:468
  51.5 2.3 %finish.1 = (bf16[512,2048]{1,0:T(8,128)(2,1)}, f32[1,1,128,128]{3,2,1,0:T(8,128)}) custom-call(f32[512,2048]{1,0:T(8,128)S(1)} %get-tuple-element.6.acc_ref, bf16[16,512,128]{2,1,0:T(8,128)(2,1)S(1)} %get-tuple-element.7.recv_ref, bf16[8,4,4,128,256]{4,3,2,1,0:T(8,128)(2,1)S(1)} %get-tuple-element.8.w_ref, f32[1,1,128,128]{3,2,1,0:T(8,128)S(1)} %get-tuple-element.9.p_ref), custom_call_target="tpu_custom_call" | custom-call | tf_op jit(solution)/shard_map/finish/pallas_call | solution.py:510
